TPU v7x, 256 devices: a whole 4x4x8 slice. The times are simulated.
256 devices in a mesh: outer: 16 (over x, z_hi), dp: 8 (over y, z_lo), mp: 2 (over core).
Axes of the slice: x: 4, y: 4, z: 8 (z_hi: 4, z_lo: 2; z = z_hi * 2 + z_lo), core: 2. Of those that a mesh axis runs over, the one named last changes fastest.
Arguments:
- step_index: int32 [], replicated, may hold values from 0 to 4095
- token_ids: int32 [16, 4096], P('outer', 'dp'), may hold values from 0 to 128255, as said below
- features: bfloat16 [16, 4096, 4096], P('outer', 'dp'), may hold values from -6 to 6
- cotangent: bfloat16 [16, 4096, 2048], P('outer', 'dp', 'mp'), may hold values from -6 to 6
- weight: float32 [16, 4096, 2048], P('outer', 'dp', 'mp'), may hold values from -0.09375 to 0.09375
- momentum: float32 [16, 4096, 2048], P('outer', 'dp', 'mp'), may hold values from -0.3 to 0.3
Outputs:
- input_grad: bfloat16 [16, 4096, 4096], P('outer', 'dp')
- new_weight: float32 [16, 4096, 2048], P('outer', 'dp', 'mp')
- new_momentum: float32 [16, 4096, 2048], P('outer', 'dp', 'mp')
Inputs may be any that keep to these rules, and one draw needn't show every extreme that they name: `token_ids`: the id 128004 marks padding at the end of some blocks of 512 tokens; a quarter of the tokens or so are padding.
All inputs are finite; a program needn't handle non-finite values.
Results may differ from a plain program's by a relative error of at most 0.0049.
Values may be sent and summed in bfloat16 or wider, within the bound.
A program may use at most 128 MiB of HBM per device.

v0:
```python
import jax
import jax.numpy as jnp
from jax import lax
from jax.sharding import PartitionSpec as P

pad_token = 128004
peak_rate = 0.1
warm_steps = 4096.0
momentum_keep = 0.9


def shortened(x):
    return jax.tree.map(lambda a: a.astype(jnp.bfloat16) if a.dtype == jnp.float32 else a, x)


def from_partner(value, axis, stride):
    mask = 2**stride
    pairs = [(source, source ^ mask) for source in range(lax.axis_size(axis))]
    return lax.ppermute(value, axis, pairs)


def swap_state(values, step_index):
    bit_count = lax.axis_size("outer").bit_length() - 1

    def make_trade(bit_index):

        def trade_with(pair):
            return jax.tree.map(
                lambda part, own: part.astype(own.dtype),
                from_partner(shortened(pair), "outer", bit_index),
                pair,
            )

        return trade_with

    return lax.switch(step_index % bit_count, [make_trade(b) for b in range(bit_count)], values)


def on_device(step_index, token_ids, features, cotangent, weight, momentum):
    activation = features[0]
    tok_rows = activation.shape[0]
    keep_mask = (token_ids[0] != pad_token)[:, None]
    masked = jnp.where(keep_mask, cotangent[0], jnp.zeros_like(cotangent[0]))
    pod_tokens = tok_rows * lax.axis_size("dp")
    master = weight[0]
    velocity_old = momentum[0]
    weight_half = master.astype(jnp.bfloat16)
    rate = peak_rate * (step_index + 1).astype(jnp.float32) / warm_steps
    partial_grad = lax.dot_general(
        masked,
        lax.all_gather(weight_half, "dp", axis=0, tiled=True),
        (((1,), (1,)), ((), ())),
        preferred_element_type=jnp.float32,
    )
    input_grad = lax.psum(partial_grad, "mp").astype(jnp.bfloat16)
    gradient = lax.psum_scatter(
        lax.dot_general(
            activation, masked, (((0,), (0,)), ((), ())), preferred_element_type=jnp.float32
        ),
        "dp",
        scatter_dimension=0,
        tiled=True,
    )
    gradient = gradient / pod_tokens
    velocity = momentum_keep * velocity_old + gradient
    stepped = master - rate * velocity
    peer_stepped, peer_velocity = swap_state((stepped, velocity), step_index)
    new_master = 0.5 * (stepped + peer_stepped)
    new_velocity = 0.5 * (velocity + peer_velocity)
    return (input_grad[None], new_master[None], new_velocity[None])


def solution(mesh):
    placed = (
        P(),
        P("outer", "dp"),
        P("outer", "dp", None),
        P("outer", "dp", "mp"),
        P("outer", "dp", "mp"),
        P("outer", "dp", "mp"),
    )
    return jax.shard_map(
        on_device,
        mesh=mesh,
        in_specs=placed,
        out_specs=(P("outer", "dp", None), P("outer", "dp", "mp"), P("outer", "dp", "mp")),
        check_vma=False,
    )
```

profile of v0, /device:TPU:1, one launch (start us, length us, event | category | flops | bytes accessed | tf_op | source)
XLA Modules:
  0.0 590.4 jit_solution(17483989321666012078)
XLA Ops:
  7.2 0.0 all-gather.2.cloned.1.call-start
  7.2 1.9 copy.9
  9.1 0.0 copy-start
  9.2 0.0 copy-start.3
  9.2 0.0 copy-start.4
  9.2 1.1 bitcast_convert_fusion
  10.3 0.0 all-gather.2.cloned.1.call-update
  10.3 0.5 copy-done
  10.8 0.0 reduce-scatter.2.cloned.1.call-start
  10.8 0.0 copy-done.3
  10.8 0.4 copy-done.4
  11.2 10.4 %convolution_bitcast_fusion = f32[4096,1024]{0,1:T(8,128)} fusion(bf16[1,512,4096]{2,1,0:T(8,128)(2,1)} %param.12, bf16[1,512,1024]{2,1,0:T(8,128)(2,1)S(1)} %copy-done.4, pred[512]{0:T(512)(128)(4,1)S(1)} %compare_reduce_fusion), kind=kOutput, calls=%fused_computation | convolution fusion | flops 4295491584 | bytes 22020608 | tf_op jit(solution)/shard_map/dot_general | solution.py:57
  21.6 0.0 reduce-scatter.2.cloned.1.call-update
  22.4 0.8 copy-done.2
  23.2 1.8 copy.10
  25.0 160.2 %all-gather.2.cloned.1.call-done = bf16[4096,1024]{0,1:T(8,128)(2,1)} async-done(((bf16[512,1024]{0,1:T(8,128)(2,1)}), bf16[4096,1024]{0,1:T(8,128)(2,1)}) %all-gather.2.cloned.1.call-update) | async-done | bytes 8388624 | tf_op jit(solution)/shard_map/all_gather | solution.py:51
  185.2 10.2 %fusion.6 = f32[512,4096]{1,0:T(8,128)} fusion(bf16[4096,1024]{0,1:T(8,128)(2,1)} %all-gather.2.cloned.1.call-done, bf16[1,512,1024]{2,1,0:T(8,128)(2,1)S(1)} %copy-done.4, pred[512]{0:T(512)(128)(4,1)S(1)} %compare_reduce_fusion), kind=kOutput, calls=%fused_computation.14 | convolution fusion | flops 4295491584 | bytes 17826304 | tf_op jit(solution)/shard_map/dot_general | solution.py:49
  195.4 26.7 %all-reduce.1 = bf16[512,4096]{1,0:T(8,128)(2,1)} all-reduce(f32[512,4096]{1,0:T(8,128)} %fusion.6), channel_id=1, replica_groups=mesh['outer'=16,'dp'=8,'mp'=2] {'mp'}, use_global_device_ids=true, to_apply=%region_0.1 | all-reduce | flops 2097152 | bytes 12582912 | tf_op jit(solution)/shard_map/psum | solution.py:55
  222.1 295.9 %reduce-scatter.2.cloned.1.call-done = f32[512,1024]{0,1:T(8,128)} async-done(((f32[4096,1024]{0,1:T(8,128)}), f32[512,1024]{0,1:T(8,128)}) %reduce-scatter.2.cloned.1.call-update) | async-done | bytes 2097168 | tf_op jit(solution)/shard_map/reduce_scatter | solution.py:56
  517.9 5.0 bitcast_subtract_fusion
  522.9 47.3 %conditional.4 = (bf16[512,1024]{1,0:T(8,128)(2,1)}, bf16[512,1024]{1,0:T(8,128)(2,1)}) conditional(s32[]{:T(128)} %clamp.3, (f32[512,1024]{0,1:T(8,128)S(1)}, f32[512,1024]{0,1:T(8,128)}) %bitcast_subtract_fusion, (f32[512,1024]{0,1:T(8,128)S(1)}, f32[512,1024]{0,1:T(8,128)}) %bitcast_subtract_fusion, ...), branch_computations={%region_2.3_spmd, %region_3.4_spmd, %region_4.5_spmd, %region_5.6_... | conditional | bytes 14680160
  522.9 0.6 copy.15
  523.5 1.3 collective-permute-start.4
  524.8 2.5 copy.16
  527.3 0.3 collective-permute-start.5
  527.6 20.2 %collective-permute-done.4 = bf16[512,1024]{1,0:T(8,128)(2,1)} collective-permute-done((bf16[512,1024]{1,0:T(8,128)(2,1)S(1)}, bf16[512,1024]{1,0:T(8,128)(2,1)}, u32[]{:S(2)}, u32[]{:S(2)}) %collective-permute-start.4) | collective-permute-done | bytes 1048608 | tf_op jit(solution)/shard_map/cond/branch_2_fun/ppermute | solution.py:19
  547.8 22.5 %collective-permute-done.5 = bf16[512,1024]{1,0:T(8,128)(2,1)} collective-permute-done((bf16[512,1024]{1,0:T(8,128)(2,1)}, bf16[512,1024]{1,0:T(8,128)(2,1)}, u32[]{:S(2)}, u32[]{:S(2)}) %collective-permute-start.5) | collective-permute-done | bytes 1048608 | tf_op jit(solution)/shard_map/cond/branch_2_fun/ppermute | solution.py:19
  570.2 1.5 copy.19
  571.8 2.3 copy.20
  574.0 4.7 fusion.2
  578.7 3.0 copy.21
  581.7 1.8 copy.22
  (4 shorter events, 0.0 us)
Async XLA Ops:
  7.2 178.1 %all-gather.2.cloned.1.call-start = ((), (), s32[]{:S(2)}) async-start(), calls=%async_computation.1 | async-start | bytes 9437184 | tf_op jit(solution)/shard_map/all_gather | solution.py:51
  9.1 1.7 copy-start
  9.2 1.7 copy-start.3
  9.2 2.0 copy-start.4
  10.8 507.1 %reduce-scatter.2.cloned.1.call-start = ((), (), s32[]{:S(2)}) async-start(), calls=%async_computation.2 | async-start | bytes 18874368 | tf_op jit(solution)/shard_map/reduce_scatter | solution.py:56
  21.6 1.6 copy-start.2
  523.5 24.3 %collective-permute-start.4 = (bf16[512,1024]{1,0:T(8,128)(2,1)S(1)}, bf16[512,1024]{1,0:T(8,128)(2,1)}, u32[]{:S(2)}, u32[]{:S(2)}) collective-permute-start(bf16[512,1024]{1,0:T(8,128)(2,1)S(1)} %copy.15), channel_id=1, source_target_pairs={{0,64},{16,80},{32,96},{48,112},{64,0},{80,16},{96,32},{112,48},{1... | collective-permute-start | bytes 3145736 | tf_op jit(solution)/shard_map/cond/branch_2_fun/ppermute | solution.py:19
  527.3 42.9 %collective-permute-start.5 = (bf16[512,1024]{1,0:T(8,128)(2,1)}, bf16[512,1024]{1,0:T(8,128)(2,1)}, u32[]{:S(2)}, u32[]{:S(2)}) collective-permute-start(bf16[512,1024]{1,0:T(8,128)(2,1)} %copy.16), channel_id=1, source_target_pairs={{0,64},{16,80},{32,96},{48,112},{64,0},{80,16},{96,32},{112,48},{1... | collective-permute-start | bytes 3145736 | tf_op jit(solution)/shard_map/cond/branch_2_fun/ppermute | solution.py:19
  578.7 3.0 copy-start.1
Sparse Core Ops, SparseCore 0:
  10.4 174.7 all-gather.1
  187.8 330.0 reduce-scatter.1
where the time goes:
time: 591 us; the launch traced here: 590 us
  waiting for transfers between devices  499 us (84%)
  blocking collectives  26.7 us (5%)
  matrix products  20.6 us (3%)
  local copies, waits for them, and re-layouts  17.1 us (3%)
  between operations  14.9 us (3%)
  other arithmetic  10.7 us (2%)
    reduce_scatter x1, waiting for transfers between devices, on_device(): lax.psum_scatter(lax.dot_general(activation, masked, (((0,), (0,)), ((),...  296 us
    all_gather x1, waiting for transfers between devices, on_device(): lax.all_gather(weight_half, 'dp', axis=0, tiled=True)  160 us
    ppermute x2, waiting for transfers between devices, from_partner(): return lax.ppermute(value, axis, pairs)  42.7 us
    psum x1, blocking collectives, on_device(): input_grad = lax.psum(partial_grad, 'mp').astype(jnp.bfloat16)  26.7 us
    unnamed x16, local copies, waits for them, and re-layouts  14 us
  transfers between devices with their start and end apart: 4, of which 4 were waited for; matrix products, arithmetic and copies ran while one was open for 4% of the time, Pallas kernels for 0%

commit v1 on v0

v1 whole, which is shorter than its diff:
```python
import functools

import jax
import jax.numpy as jnp
from jax import lax
from jax.experimental import pallas as pl
from jax.experimental.pallas import tpu as pltpu
from jax.sharding import PartitionSpec as P

pad_token = 128004
peak_rate = 0.1
warm_steps = 4096.0
momentum_keep = 0.9

MESH = pl.DeviceIdType.MESH
BF16 = jnp.bfloat16
F32 = jnp.float32
NY = 4
NX = 4


def body(
    bit,
    rate_ref,
    feat,
    masked,
    whalf,
    weight,
    momentum,
    grad_out,
    w_out,
    v_out,
    m_buf,
    f_buf,
    ft_buf,
    w_pair,
    rs_send,
    rs_recv,
    g_own,
    w_own,
    v_own,
    w_peer,
    v_send,
    v_peer,
    i_keep,
    i_send,
    i_recv,
    o_fin,
    o_recv,
    loc,
    snd,
    rcv,
):
    outer, dp, c = lax.axis_index("outer"), lax.axis_index("dp"), lax.axis_index("mp")
    x, zh = outer // NX, outer % NX
    y, zl = dp // 2, dp % 2
    tok, hw = masked.shape
    half = tok // 2
    blk = whalf.shape[0]
    nk = f_buf.shape[0]
    sub = f_buf.shape[2]
    nq = nk // 2

    def at_y(step):
        return (outer, ((y + step + NY) % NY) * 2 + zl, c)

    z_peer = (outer, y * 2 + 1 - zl, c)
    core_peer = (outer, dp, 1 - c)
    if bit == 0:
        other = x * 4 + zh + 1 - 2 * (zh % 2)
    elif bit == 1:
        other = x * 4 + (zh + 2) % 4
    elif bit == 2:
        other = (x + 1 - 2 * (x % 2)) * 4 + zh
    else:
        other = ((x + 2) % 4) * 4 + zh
    peer = (other, dp, c)

    count = {"loc": 0, "rem": 0}

    def local(src, dst):
        i = count["loc"]
        count["loc"] += 1
        copy = pltpu.make_async_copy(src, dst, loc.at[i])
        copy.start()
        return copy

    pending = []

    def remote(src, dst, to):
        i = count["rem"]
        count["rem"] += 1
        copy = pltpu.make_async_remote_copy(
            src_ref=src,
            dst_ref=dst,
            send_sem=snd.at[i],
            recv_sem=rcv.at[i],
            device_id=to,
            device_id_type=MESH,
        )
        copy.start()
        pending.append(copy)
        return copy

    in_m = local(masked, m_buf.at[pl.ds(0, tok)])
    in_w = local(whalf, w_pair.at[zl])

    barrier = pltpu.get_barrier_semaphore()
    partners = (at_y(1), at_y(-1), at_y(2), z_peer, core_peer, peer)
    for to in partners:
        pl.semaphore_signal(barrier, inc=1, device_id=to, device_id_type=MESH)
    pl.semaphore_wait(barrier, len(partners))

    lo, hi = pl.ds(0, half), pl.ds(half, half)

    def rows(r, part):
        return pl.ds(r * tok + part * half, half)

    up_a = remote(masked.at[lo], m_buf.at[rows(3, 0)], at_y(1))
    dn_b = remote(masked.at[hi], m_buf.at[rows(1, 1)], at_y(-1))
    up_b = remote(masked.at[hi], m_buf.at[rows(3, 1)], at_y(1))
    dn_a = remote(masked.at[lo], m_buf.at[rows(1, 0)], at_y(-1))
    pair = remote(whalf, w_pair.at[zl], z_peer)
    w_swap = remote(whalf, w_peer, peer)

    def columns(ychip, k):
        j = (1 - zl) if k < nq else zl
        return pl.ds(pl.multiple_of(ychip * 2 * blk + j * blk + (k % nq) * sub, sub), sub)

    in_f = [local(feat.at[:, columns(y, k)], f_buf.at[k, pl.ds(0, tok)]) for k in range(nk)]
    in_v = local(momentum, v_own)
    in_wf = local(weight, w_own)

    up_a.wait_recv()
    fwd_up = remote(m_buf.at[rows(3, 0)], m_buf.at[rows(2, 0)], at_y(1))
    dn_b.wait_recv()
    fwd_dn = remote(m_buf.at[rows(1, 1)], m_buf.at[rows(2, 1)], at_y(-1))

    mine = pl.ds(pl.multiple_of(c * half, half), half)

    def f_rows(r):
        return pl.ds(pl.multiple_of(r * tok + c * half, half), half)

    f_in = {}
    for k in range(nk):
        for step, slot in ((1, 3), (-1, 1), (2, 2)):
            f_in[k, slot] = remote(
                feat.at[mine, columns((y + step + NY) % NY, k)],
                f_buf.at[k, f_rows(slot)],
                at_y(step),
            )

    nt = blk // 2

    def partial_terms(r):
        def one(t, carry):
            j, n = t // 2, t % 2
            part = lax.dot_general(
                m_buf[pl.ds(r * tok, tok), :],
                w_pair[(c + j) % 2, pl.ds(pl.multiple_of(n * nt, nt), nt), :],
                (((1,), (1,)), ((), ())),
                preferred_element_type=F32,
            )
            cols = pl.ds(pl.multiple_of(n * nt, nt), nt)

            @pl.when(j == 0)
            def _():
                i_keep[r, :, cols] = part

            @pl.when(j == 1)
            def _():
                i_send[r, :, cols] = part.astype(BF16)

            return carry

        lax.fori_loop(0, 4, one, 0)
        return remote(i_send.at[r], i_recv.at[r], core_peer)

    def finished(r, copy):
        copy.wait_recv()

        def one(t, carry):
            part = pl.ds(pl.multiple_of(t * 64, 64), 64)
            o_fin[r, part, :] = (i_keep[r, part, :] + i_recv[r, part, :].astype(F32)).astype(BF16)
            return carry

        lax.fori_loop(0, tok // 64, one, 0)

    def out_columns(ychip):
        return pl.ds(pl.multiple_of(ychip * 2 * blk + c * blk, blk), blk)

    out_stores, out_in = [], []

    def spread(src, ychip):
        out_stores.append(local(src, grad_out.at[:, out_columns(ychip)]))
        out_in.append(remote(src, grad_out.at[:, out_columns(ychip)], core_peer))

    in_m.wait()
    in_w.wait()
    pair.wait_recv()
    p0 = partial_terms(0)
    up_b.wait_recv()
    p3 = partial_terms(3)
    dn_a.wait_recv()
    p1 = partial_terms(1)
    o_in = {}
    finished(3, p3)
    o_in[1] = remote(o_fin.at[3], o_recv.at[0], at_y(-1))
    finished(1, p1)
    o_in[3] = remote(o_fin.at[1], o_recv.at[2], at_y(1))
    finished(0, p0)
    spread(o_fin.at[0], y)

    fwd_up.wait_recv()
    fwd_dn.wait_recv()
    p2 = partial_terms(2)

    hn = hw // 4
    rs_in, v_in = [], []
    for k in range(nk):
        in_f[k].wait()
        shared = []
        for slot in (3, 1, 2):
            f_in[k, slot].wait_recv()
            shared.append(remote(f_buf.at[k, f_rows(slot)], f_buf.at[k, f_rows(slot)], core_peer))
        for copy in shared:
            copy.wait_recv()

        def turn(t, carry):
            part = pl.ds(pl.multiple_of(t * tok, tok), tok)
            ft_buf[:, part] = f_buf[k, part, :].T
            return carry

        lax.fori_loop(0, NY, turn, 0)

        def one(n, carry):
            cols = pl.ds(pl.multiple_of(n * hn, hn), hn)
            part = jnp.dot(ft_buf[...], m_buf[:, cols], preferred_element_type=F32)
            if k < nq:
                rs_send[k, :, cols] = part.astype(BF16)
            else:
                g_own[:, cols] = part
            return carry

        lax.fori_loop(0, 4, one, 0)
        if k < nq:
            rs_in.append(remote(rs_send.at[k], rs_recv.at[k], z_peer))
            if k == 0:
                finished(2, p2)
                o_in[2] = remote(o_fin.at[2], o_recv.at[1], at_y(2))
            continue
        q = k - nq
        if q == 0:
            in_v.wait()
        rs_in[q].wait_recv()

        def move(t, carry):
            part = pl.ds(pl.multiple_of(t * 32, 32), 32)
            own = pl.ds(pl.multiple_of(q * sub + t * 32, 32), 32)
            grad = (g_own[part, :] + rs_recv[q, part, :].astype(F32)) * (1.0 / (NY * 2 * tok))
            vel = momentum_keep * v_own[own, :] + grad
            v_own[own, :] = vel
            v_send[q, part, :] = vel.astype(BF16)
            return carry

        lax.fori_loop(0, sub // 32, move, 0)
        v_in.append(remote(v_send.at[q], v_peer.at[q], peer))

    def spread_arrived():
        for slot in (1, 3, 2):
            o_in[slot].wait_recv()
            spread(o_recv.at[slot - 1], (y + slot) % NY)

    if bit < 2:
        spread_arrived()
    rate = rate_ref[0]
    in_wf.wait()
    w_swap.wait_recv()
    results = []
    for q in range(nq):
        v_in[q].wait_recv()

        def final(t, carry):
            part = pl.ds(pl.multiple_of(t * 32, 32), 32)
            own = pl.ds(pl.multiple_of(q * sub + t * 32, 32), 32)
            vel = 0.5 * (v_own[own, :] + v_peer[q, part, :].astype(F32))
            v_own[own, :] = vel
            w_own[own, :] = 0.5 * (w_own[own, :] + w_peer[own, :].astype(F32)) - rate * vel
            return carry

        lax.fori_loop(0, sub // 32, final, 0)
        own = pl.ds(q * sub, sub)
        results.append(local(v_own.at[own], v_out.at[own]))
        results.append(local(w_own.at[own], w_out.at[own]))
    if bit >= 2:
        spread_arrived()
    for copy in out_in:
        copy.wait_recv()
    for copy in pending:
        copy.wait_send()
    for copy in results + out_stores:
        copy.wait()


def make_call(bit, tok, width, blk, hw, subs=4):
    sub = 2 * blk // subs
    any_space = pl.BlockSpec(memory_space=pl.ANY)
    flops = 4 * tok * width * hw
    return pl.pallas_call(
        functools.partial(body, bit),
        name=f"pod_step_{bit}",
        out_shape=(
            jax.ShapeDtypeStruct((tok, width), BF16),
            jax.ShapeDtypeStruct((blk, hw), F32),
            jax.ShapeDtypeStruct((blk, hw), F32),
        ),
        in_specs=[pl.BlockSpec(memory_space=pltpu.SMEM)] + [any_space] * 5,
        out_specs=(any_space, any_space, any_space),
        scratch_shapes=[
            pltpu.VMEM((NY * tok, hw), BF16),
            pltpu.VMEM((subs, NY * tok, sub), BF16),
            pltpu.VMEM((sub, NY * tok), BF16),
            pltpu.VMEM((2, blk, hw), BF16),
            pltpu.VMEM((subs // 2, sub, hw), BF16),
            pltpu.VMEM((subs // 2, sub, hw), BF16),
            pltpu.VMEM((sub, hw), F32),
            pltpu.VMEM((blk, hw), F32),
            pltpu.VMEM((blk, hw), F32),
            pltpu.VMEM((blk, hw), BF16),
            pltpu.VMEM((subs // 2, sub, hw), BF16),
            pltpu.VMEM((subs // 2, sub, hw), BF16),
            pltpu.VMEM((NY, tok, blk), F32),
            pltpu.VMEM((NY, tok, blk), BF16),
            pltpu.VMEM((NY, tok, blk), BF16),
            pltpu.VMEM((NY, tok, blk), BF16),
            pltpu.VMEM((NY - 1, tok, blk), BF16),
            pltpu.SemaphoreType.DMA((64,)),
            pltpu.SemaphoreType.DMA((96,)),
            pltpu.SemaphoreType.DMA((96,)),
        ],
        compiler_params=pltpu.CompilerParams(
            collective_id=bit, has_side_effects=True, vmem_limit_bytes=60 * 1024 * 1024
        ),
        cost_estimate=pl.CostEstimate(flops=flops, bytes_accessed=32 << 20, transcendentals=0),
    )


def on_device(step_index, token_ids, features, cotangent, weight, momentum):
    feat = features[0]
    tok, width = feat.shape
    blk, hw = weight.shape[1:]
    keep_mask = (token_ids[0] != pad_token)[:, None]
    masked = jnp.where(keep_mask, cotangent[0], jnp.zeros_like(cotangent[0]))
    whalf = weight[0].astype(BF16)
    rate = peak_rate * (step_index + 1).astype(F32) / warm_steps
    bit_count = lax.axis_size("outer").bit_length() - 1
    calls = [make_call(b, tok, width, blk, hw) for b in range(bit_count)]
    operands = (rate[None], feat, masked, whalf, weight[0], momentum[0])
    input_grad, new_master, new_velocity = lax.switch(
        step_index % bit_count, [lambda *a, call=call: call(*a) for call in calls], *operands
    )
    return (input_grad[None], new_master[None], new_velocity[None])


def solution(mesh):
    placed = (
        P(),
        P("outer", "dp"),
        P("outer", "dp", None),
        P("outer", "dp", "mp"),
        P("outer", "dp", "mp"),
        P("outer", "dp", "mp"),
    )
    return jax.shard_map(
        on_device,
        mesh=mesh,
        in_specs=placed,
        out_specs=(P("outer", "dp", None), P("outer", "dp", "mp"), P("outer", "dp", "mp")),
        check_vma=False,
    )
```

time: 591 us -> 144 us (0.24)
  waiting for transfers between devices: 499 us -> 0 us
  Pallas kernels: 0 us -> 130 us
  blocking collectives: 26.7 us -> 0 us
  matrix products: 20.6 us -> 0 us
  between operations: 14.9 us -> 1.31 us
  local copies, waits for them, and re-layouts: 17.1 us -> 8.52 us
  other arithmetic: 10.7 us -> 4.32 us
    reduce_scatter x1 -> x0, waiting for transfers between devices: 296 us -> none  [on_device(): lax.psum_scatter(lax.dot_general(activation, masked, (((0,), (0,)), ((),...]
    all_gather x1 -> x0, waiting for transfers between devices: 160 us -> none  [on_device(): lax.all_gather(weight_half, 'dp', axis=0, tiled=True)]
    pallas_call x0 -> x1, Pallas kernels: none -> 130 us  [on_device(): call(*a)]
    ppermute x2 -> x0, waiting for transfers between devices: 42.7 us -> none  [from_partner(): return lax.ppermute(value, axis, pairs)]
    psum x1 -> x0, blocking collectives: 26.7 us -> none  [on_device(): input_grad = lax.psum(partial_grad, 'mp').astype(jnp.bfloat16)]
    dot_general x2 -> x0, matrix products: 20.6 us -> none  [the longest x1 10.4 us: on_device(): lax.dot_general(activation, masked, (((0,), (0,)), ((), ())), preferred_e...]
    unnamed x16 -> x7, local copies, waits for them, and re-layouts: 14 us -> 8.52 us
  transfers between devices with their start and end apart: 4 -> 0, of which waited for: 4 -> 0; matrix products, arithmetic and copies ran while one was open for 4% -> 0% of each run, Pallas kernels for 0% -> 0%
where the time goes in v1:
time: 144 us
  Pallas kernels  130 us (90%)
  local copies, waits for them, and re-layouts  8.52 us (6%)
  other arithmetic  4.32 us (3%)
    pallas_call x1, Pallas kernels, on_device(): call(*a)  130 us
    unnamed x7, local copies, waits for them, and re-layouts  8.52 us

profile of v1, /device:TPU:1, one launch (start us, length us, event | category | flops | bytes accessed | tf_op | source)
XLA Modules:
  0.0 144.1 jit_solution(18327982992844794409)
XLA Ops:
  1.3 134.2 %conditional.1 = ((bf16[512,4096]{1,0:T(8,128)(2,1)}, f32[512,1024]{1,0:T(8,128)}, f32[512,1024]{1,0:T(8,128)})) conditional(s32[]{:T(128)} %clamp.3, (f32[]{:T(128)}, bf16[1,512,4096]{2,1,0:T(8,128)(2,1)}, s32[1,512]{1,0:T(1,128)}, bf16[1,512,1024]{2,1,0:T(8,128)(2,1)}, f32[512,1024]{1,0:T(8,128)}, ...), branch_computations={%region_0.1_spmd, %region_1.2_spmd, %region_2.3_spmd, %region_3.4_... | conditional | flops 8590984192 | bytes 47189040 | solution.py:359
  1.3 0.0 copy-start
  1.3 0.9 compare_reduce_fusion
  2.2 2.3 %bitcast_select_fusion.masked = bf16[512,1024]{1,0:T(8,128)(2,1)} fusion(bf16[1,512,1024]{2,1,0:T(8,128)(2,1)} %get-tuple-element.198, pred[512]{0:T(512)(128)(4,1)S(1)} %compare_reduce_fusion), kind=kLoop, calls=%fused_computation | loop fusion | flops 524288 | bytes 2097664 | tf_op jit(solution)/shard_map/jit(_where)/select_n | solution.py:353
  4.5 0.0 copy-done
  4.5 1.1 convert_element_type.15.whalf
  5.6 129.6 %pod_step_0.2 = (bf16[512,4096]{1,0:T(8,128)(2,1)}, f32[512,1024]{1,0:T(8,128)}, f32[512,1024]{1,0:T(8,128)}) custom-call(f32[1]{0:T(128)} %bitcast.rate_ref, bf16[512,4096]{1,0:T(8,128)(2,1)} %bitcast.31, bf16[512,1024]{1,0:T(8,128)(2,1)} %bitcast_select_fusion.masked, bf16[512,1024]{1,0:T(8,128)(2,1)} %convert_element_type.15.whalf, ...), custom_call_target="tpu_custom_call" | custom-call | flops 8589934592 | bytes 33554432 | tf_op jit(solution)/shard_map/cond/branch_0_fun/pod_step_0/pallas_call | solution.py:360
  135.5 0.0 copy-start.4
  135.5 4.8 %copy.25 = bf16[1,512,4096]{2,1,0:T(8,128)(2,1)} copy(bf16[1,512,4096]{2,1,0:T(8,128)(2,1)} %bitcast.28) | data formatting | bytes 8388608
  140.4 0.0 copy-done.4
  140.4 0.0 copy-start.5
  140.4 1.3 copy.26
  141.7 1.0 copy-done.5
  142.7 1.3 copy.27
Async XLA Ops:
  1.3 3.2 %copy-start = (f32[512,1024]{1,0:T(8,128)S(1)}, f32[512,1024]{1,0:T(8,128)}, u32[]{:S(2)}) copy-start(f32[512,1024]{1,0:T(8,128)} %get-tuple-element.199.weight) | copy-start | bytes 6291460 | tf_op jit(solution)/shard_map/cond
  135.5 4.9 %copy-start.4 = (f32[512,1024]{1,0:T(8,128)S(1)}, f32[512,1024]{1,0:T(8,128)}, u32[]{:S(2)}) copy-start(f32[512,1024]{1,0:T(8,128)} %get-tuple-element.236) | copy-start | bytes 6291460
  140.4 2.3 %copy-start.5 = (f32[512,1024]{1,0:T(8,128)S(1)}, f32[512,1024]{1,0:T(8,128)}, u32[]{:S(2)}) copy-start(f32[512,1024]{1,0:T(8,128)} %get-tuple-element.235) | copy-start | bytes 6291460
